TPU v7x, 32 devices: a whole 2x2x4 slice. The times are simulated.
32 devices in a mesh: seq: 8 (over y, x, core), seg: 4 (over z).
Axes of the slice: x: 2, y: 2, z: 4, core: 2. Of those that a mesh axis runs over, the one named last changes fastest.
Arguments:
- query_rows: bfloat16 [4, 2048, 4, 128], P('seg', 'seq'), may hold values from -6 to 6
- key_rows: bfloat16 [4, 2048, 2, 4, 128], P('seg', 'seq'), may hold values from -6 to 6
- value_rows: bfloat16 [4, 2048, 2, 4, 128], P('seg', 'seq'), may hold values from -6 to 6
- out_gain: float32 [4, 128], replicated, may hold values from 0.5 to 1.5
- initial_state: float32 [4, 128, 128], replicated, may hold values from -24 to 24
Outputs:
- normed_out: bfloat16 [4, 2048, 4, 128], P('seg', 'seq')
All inputs are finite; a program needn't handle non-finite values.
Results may differ from a plain program's by a relative error of at most 0.004.
Values sent between devices are 32-bit elements; how exact they have to be, the bound alone decides.
A program may use at most 128 MiB of HBM per device.

v0:
```python
import jax
import jax.numpy as jnp
from jax import lax
from jax.sharding import PartitionSpec as P

DK = 128
DV = 128
HEADS = 4
REFL = 2
GROUP = 128
highest = lax.Precision.HIGHEST


def carried_in(part, axis, combine, identity):
    place = lax.axis_index(axis)
    gathered = lax.all_gather(part, axis)
    state = jnp.zeros_like(part) + jnp.asarray(identity, part.dtype)

    def one(step, state):
        return combine(state, lax.dynamic_index_in_dim(gathered, step, 0, False))

    return lax.fori_loop(0, place, one, state)


def unit_keys(raw):
    raw = raw.astype(jnp.float32)
    return raw * lax.rsqrt(jnp.sum(raw * raw, axis=-1, keepdims=True) + 1e-06)


def solve_single(matrix, target):
    return jax.scipy.linalg.solve_triangular(matrix, target, lower=True, unit_diagonal=True)


def block_factors(query, keyed, valued):
    steps = keyed.shape[-2]
    tokens = query.shape[-2]
    key_gram = jnp.einsum("...id,...jd->...ij", keyed, keyed, precision=highest)
    lower_unit = jnp.eye(steps, dtype=jnp.float32) + jnp.tril(2.0 * key_gram, -1)
    target = jnp.concatenate([2.0 * keyed, 2.0 * valued], axis=-1)
    flat_lower = lower_unit.reshape(-1, steps, steps)
    flat_target = target.reshape(-1, steps, target.shape[-1])
    solved = jax.vmap(solve_single)(flat_lower, flat_target).reshape(target.shape)
    weights = solved[..., : keyed.shape[-1]]
    updates = solved[..., keyed.shape[-1] :]
    visible = jnp.arange(steps)[None, :] <= REFL * jnp.arange(tokens)[:, None] + (REFL - 1)
    scores = jnp.where(
        visible, jnp.einsum("...td,...ld->...tl", query, keyed, precision=highest), 0.0
    )
    return (weights, updates, scores)


def compose(first_pair, second_pair):
    second_trans = second_pair[..., :DK]
    moved = jnp.einsum("...de,...ef->...df", second_trans, first_pair, precision=highest)
    added = jnp.concatenate([jnp.zeros_like(second_trans), second_pair[..., DK:]], axis=-1)
    return moved + added


def identity_pair():
    eye_part = jnp.broadcast_to(jnp.eye(DK, dtype=jnp.float32), (HEADS, DK, DK))
    return jnp.concatenate([eye_part, jnp.zeros((HEADS, DK, DV), jnp.float32)], axis=-1)


def apply_pair(pair, state):
    return jnp.einsum("hde,hef->hdf", pair[..., :DK], state, precision=highest) + pair[..., DK:]


def ordered_prefix(stacked, position):

    def ordered_accumulate(carry, piece):
        return (compose(carry, piece), carry)

    closing, before_all = lax.scan(ordered_accumulate, identity_pair(), stacked)
    return (lax.dynamic_index_in_dim(before_all, position, 0, keepdims=False), closing)


def per_device(query_rows, key_rows, value_rows, out_gain, initial_state):
    tokens = query_rows.shape[1]
    nblock = tokens // GROUP
    query = (
        query_rows[0].astype(jnp.float32).reshape(nblock, GROUP, HEADS, DK).transpose(0, 2, 1, 3)
    )
    keyed = unit_keys(key_rows[0]).reshape(nblock, GROUP * REFL, HEADS, DK).transpose(0, 2, 1, 3)
    valued = (
        value_rows[0]
        .astype(jnp.float32)
        .reshape(nblock, GROUP * REFL, HEADS, DV)
        .transpose(0, 2, 1, 3)
    )
    weights, updates, scores = block_factors(query, keyed, valued)
    trans_block = jnp.eye(DK, dtype=jnp.float32) - jnp.einsum(
        "chld,chle->chde", keyed, weights, precision=highest
    )
    state_block = jnp.einsum("chld,chle->chde", keyed, updates, precision=highest)
    block_pairs = jnp.concatenate([trans_block, state_block], axis=-1)
    project = query - jnp.einsum("chtl,chld->chtd", scores, weights, precision=highest)
    local_read = jnp.einsum("chtl,chle->chte", scores, updates, precision=highest)

    def body_accumulate(carry, piece):
        return (compose(carry, piece), carry)

    own_pair, before = lax.scan(body_accumulate, identity_pair(), block_pairs)
    reach = jnp.einsum("chtd,chde->chte", project, before[..., :DK], precision=highest)
    base_read = (
        jnp.einsum("chtd,chde->chte", project, before[..., DK:], precision=highest) + local_read
    )
    stacked = lax.all_gather(own_pair[None], "seq", axis=0, tiled=True)
    seq_before, seg_total = ordered_prefix(stacked, lax.axis_index("seq"))
    seg_before = carried_in(seg_total, "seg", compose, identity_pair())
    entry_state = apply_pair(seg_before, initial_state)
    incoming = apply_pair(seq_before, entry_state)
    reads = jnp.einsum("chtd,hde->chte", reach, incoming, precision=highest) + base_read
    reads = reads.transpose(0, 2, 1, 3).reshape(1, tokens, HEADS, DV)
    scale = lax.rsqrt(jnp.mean(reads * reads, axis=-1, keepdims=True) + 1e-06)
    return (reads * scale * out_gain).astype(jnp.bfloat16)


def solution(mesh):
    return jax.shard_map(
        per_device,
        mesh=mesh,
        in_specs=(
            P("seg", "seq", None, None),
            P("seg", "seq", None, None, None),
            P("seg", "seq", None, None, None),
            P(),
            P(),
        ),
        out_specs=P("seg", "seq", None, None),
        check_vma=False,
    )
```

profile of v0, /device:TPU:25, one launch (start us, length us, event | category | flops | bytes accessed | tf_op | source)
XLA Modules:
  0.0 318.8 jit_solution(12129353922683288932)
XLA Ops:
  7.4 1.8 multiply_reduce_fusion
  11.0 1.3 bitcast_multiply_fusion
  12.3 2.3 select_add_fusion
  15.0 5.8 %while.38 = (s32[]{:T(128)}, f32[8,256,256]{2,1,0:T(8,128)S(1)}, s32[2,2]{1,0:T(2,128)S(1)}, f32[2,8,128,128]{3,2,0,1:T(8,128)}, s32[]{:T(128)}) while((s32[]{:T(128)}, f32[8,256,256]{2,1,0:T(8,128)S(1)}, s32[2,2]{1,0:T(2,128)S(1)}, f32[2,8,128,128]{3,2,0,1:T(8,128)}, s32[]{:T(128)}) %tuple.63), condition=%wide.while_cond, body=%wide.while_body.sunk | while | flops 2 | bytes 1049709 | solution.py:31
  15.7 2.2 bitcast_dynamic-update-slice_fusion.8
  18.5 2.2 bitcast_dynamic-update-slice_fusion.8
  20.8 158.6 %custom-call.4 = f32[8,2,128,128]{2,3,1,0:T(8,128)} custom-call(f32[8,2,128,128]{3,2,1,0:T(8,128)} %bitcast.120), custom_call_target="InvertDiagBlocksLowerTriangular" | custom-call | tf_op jit(solution)/shard_map/vmap(jit(_solve_triangular))/triangular_solve | solution.py:31
  179.4 1.8 pad_maximum_fusion
  181.3 1.1 fusion.8
  183.4 1.1 fusion.22
  184.7 2.2 convolution_subtract_fusion.2
  186.9 2.2 fusion.13
  191.0 9.2 %while.35 = (s32[]{:T(128)}, f32[4,128,256]{2,1,0:T(8,128)}, f32[2,4,128,256]{3,2,1,0:T(8,128)}, f32[2,4,128,256]{2,3,1,0:T(8,128)}, s32[]{:T(128)}) while((s32[]{:T(128)}, f32[4,128,256]{2,1,0:T(8,128)}, f32[2,4,128,256]{3,2,1,0:T(8,128)}, f32[2,4,128,256]{2,3,1,0:T(8,128)}, s32[]{:T(128)}) %tuple.66), condition=%wide.region_2.3_spmd, body=%wide.region_1.2_spmd.sunk | while | flops 201457664 | bytes 6291533 | solution.py:102
  194.2 1.4 convolution_add_fusion.9
  198.8 1.4 convolution_add_fusion.9
  200.3 38.0 %all-gather.5.cloned.1.call-done = f32[32,128,256]{2,1,0:T(8,128)} async-done(((f32[4,128,256]{2,1,0:T(8,128)}), f32[32,128,256]{2,1,0:T(8,128)}) %all-gather.5.cloned.1.call-update) | async-done | bytes 4194320 | tf_op jit(solution)/shard_map/all_gather | solution.py:107
  238.4 21.0 %while.36 = (s32[]{:T(128)}, f32[4,128,256]{2,1,0:T(8,128)S(1)}, f32[8,4,128,256]{3,2,1,0:T(8,128)}, f32[8,4,128,256]{3,2,1,0:T(8,128)}, s32[]{:T(128)}) while((s32[]{:T(128)}, f32[4,128,256]{2,1,0:T(8,128)S(1)}, f32[8,4,128,256]{3,2,1,0:T(8,128)}, f32[8,4,128,256]{3,2,1,0:T(8,128)}, s32[]{:T(128)}) %tuple.80), condition=%wide.region_4.5_spmd, body=%wide.region_3.4_spmd.sunk | while | flops 201457664 | bytes 5242957 | solution.py:73
  238.4 1.1 dynamic-slice_bitcast_fusion.5
  241.0 1.1 dynamic-slice_bitcast_fusion.5
  243.7 1.1 dynamic-slice_bitcast_fusion.5
  246.3 1.1 dynamic-slice_bitcast_fusion.5
  248.9 1.1 dynamic-slice_bitcast_fusion.5
  251.5 1.1 dynamic-slice_bitcast_fusion.5
  261.8 2.8 convolution_subtract_fusion.1
  265.9 1.9 fusion.5
  267.8 1.1 dynamic-slice_bitcast_fusion.2
  268.9 34.9 %all-gather.7.cloned.1.call-done = f32[16,128,256]{2,1,0:T(8,128)} async-done(((f32[4,128,256]{2,1,0:T(8,128)}), f32[16,128,256]{2,1,0:T(8,128)}) %all-gather.7.cloned.1.call-update) | async-done | bytes 2097168 | tf_op jit(solution)/shard_map/all_gather | solution.py:16
  303.8 5.3 %while.37 = (s32[]{:T(128)}, f32[4,128,256]{2,1,0:T(8,128)S(1)}, s32[]{:T(128)}, f32[4,4,128,256]{3,2,1,0:T(8,128)}, s32[]{:T(128)}, /*index=5*/s32[]{:T(128)}, s32[]{:T(128)}) while((s32[]{:T(128)}, f32[4,128,256]{2,1,0:T(8,128)S(1)}, s32[]{:T(128)}, f32[4,4,128,256]{3,2,1,0:T(8,128)}, s32[]{:T(128)}, /*index=5*/s32[]{:T(128)}, ...), condition=%wide.region_6.7_spmd, body=%wide.region_5.6_spmd.sunk | while | flops 201457664 | bytes 4194427 | solution.py:22
  303.8 1.1 dynamic-slice_bitcast_fusion.6
  305.6 1.1 dynamic-slice_bitcast_fusion.6
  307.4 1.1 dynamic-slice_bitcast_fusion.6
  310.8 1.1 fusion.26
  (116 shorter events, 35.2 us)
Async XLA Ops:
  6.5 302.6 %copy-start = (f32[4,128,128]{2,1,0:T(8,128)S(1)}, f32[4,128,128]{2,1,0:T(8,128)}, u32[]{:S(2)}) copy-start(f32[4,128,128]{2,1,0:T(8,128)} %param.15) | copy-start | bytes 786436
  6.5 3.1 copy-start.4
  6.5 3.2 copy-start.9
  6.5 231.8 %all-gather.5.cloned.1.call-start = ((), (), s32[]{:S(2)}) async-start(), calls=%async_computation | async-start | bytes 4718592 | tf_op jit(solution)/shard_map/all_gather | solution.py:107
  12.3 2.3 copy-start.7
  179.4 1.9 copy-start.6
  184.7 4.4 %copy-start.2 = (f32[8,256,256]{2,1,0:T(8,128)}, f32[8,256,256]{2,1,0:T(8,128)S(1)}, u32[]{:S(2)}) copy-start(f32[8,256,256]{2,1,0:T(8,128)S(1)} %pad_maximum_fusion.1) | copy-start | bytes 6291460
  200.2 103.6 %all-gather.7.cloned.1.call-start = ((), (), s32[]{:S(2)}) async-start(), calls=%async_computation.1 | async-start | bytes 2621440 | tf_op jit(solution)/shard_map/all_gather | solution.py:16
  238.4 21.9 %copy-start.8 = (bf16[1,256,4,128]{3,2,1,0:T(4,128)(2,1)S(1)}, bf16[1,256,4,128]{3,2,1,0:T(4,128)(2,1)}, u32[]{:S(2)}) copy-start(bf16[1,256,4,128]{3,2,1,0:T(4,128)(2,1)} %param.11) | copy-start | bytes 786436
  259.3 0.8 copy-start.1
  260.2 1.6 copy-start.3
  260.2 4.3 %copy-start.5 = (f32[2,4,128,256]{3,2,1,0:T(8,128)S(1)}, f32[2,4,128,256]{3,2,1,0:T(8,128)}, u32[]{:S(2)}) copy-start(f32[2,4,128,256]{3,2,1,0:T(8,128)} %get-tuple-element.78) | copy-start | bytes 3145732
  309.1 1.7 copy-start.10
Sparse Core Ops, SparseCore 0:
  200.4 37.9 all-gather.4
  260.3 43.4 all-gather.6
where the time goes:
time: 320 us; the launch traced here: 319 us
  other arithmetic  168 us (52%)
  waiting for transfers between devices  73 us (23%)
  local copies, waits for them, and re-layouts  36.5 us (11%)
  matrix products  27.3 us (9%)
  between operations  13.8 us (4%)
    another operation x7, other arithmetic, solve_single(): jax.scipy.linalg.solve_triangular(matrix, target, lower=True, unit_diagon...  160 us
    all_gather x1, waiting for transfers between devices, per_device(): stacked = lax.all_gather(own_pair[None], 'seq', axis=0, tiled=True)  38 us
    all_gather x1, waiting for transfers between devices, carried_in(): gathered = lax.all_gather(part, axis)  34.9 us
    dot_general x13, matrix products, compose(): jnp.einsum('...de,...ef->...df', second_trans, first_pair, precision=high...  9.21 us
    squeeze x8, local copies, waits for them, and re-layouts, ordered_prefix(): closing, before_all = lax.scan(ordered_accumulate, identity_pair(), stacked)  8.7 us
    dynamic_update_slice x8, local copies, waits for them, and re-layouts, ordered_prefix(): closing, before_all = lax.scan(ordered_accumulate, identity_pair(), stacked)  6.85 us
  transfers between devices with their start and end apart: 2, of which 2 were waited for; matrix products, arithmetic and copies ran while one was open for 2% of the time, Pallas kernels for 0%

commit v1 on v0

--- a/solution.py
+++ b/solution.py
@@ -9,6 +9,17 @@
 REFL = 2
 GROUP = 128
 highest = lax.Precision.HIGHEST
+
+
+def fill_spot(slab_in, join_dim, dev_axis):
+    slots = lax.psum(1, dev_axis)
+    cards = [slab_in]
+    for num in range(slots - 1):
+        built = lax.ppermute(cards[-1], dev_axis, [(kk, (kk + 1) % slots) for kk in range(slots)])
+        cards.append(built)
+    main = jnp.concatenate(cards[::-1], axis=join_dim)
+    r1 = lax.axis_index(dev_axis)
+    return jnp.roll(main, (r1 + 1) * slab_in.shape[join_dim], axis=join_dim)
 
 
 def carried_in(part, axis, combine, identity):
@@ -104,7 +115,7 @@
     base_read = (
         jnp.einsum("chtd,chde->chte", project, before[..., DK:], precision=highest) + local_read
     )
-    stacked = lax.all_gather(own_pair[None], "seq", axis=0, tiled=True)
+    stacked = fill_spot(own_pair[None], 0, "seq")
     seq_before, seg_total = ordered_prefix(stacked, lax.axis_index("seq"))
     seg_before = carried_in(seg_total, "seg", compose, identity_pair())
     entry_state = apply_pair(seg_before, initial_state)

time: 320 us -> 361 us (1.13)
  starting transfers between devices: 0.04 us -> 16.8 us
  waiting for transfers between devices: 73 us -> 84 us
  local copies, waits for them, and re-layouts: 36.5 us -> 46.2 us
    ppermute x0 -> x7, waiting for transfers between devices: none -> 43.2 us  [fill_spot(): lax.ppermute(cards[-1], dev_axis, [(kk, (kk + 1) % slots) for kk in range...]
    all_gather x1 -> x0, waiting for transfers between devices: 38 us -> none  [per_device(): stacked = lax.all_gather(own_pair[None], 'seq', axis=0, tiled=True)]
    ppermute x0 -> x7, starting transfers between devices: none -> 16.8 us  [fill_spot(): lax.ppermute(cards[-1], dev_axis, [(kk, (kk + 1) % slots) for kk in range...]
    unnamed x24 -> x50, local copies, waits for them, and re-layouts: 2.51 us -> 10.2 us
    all_gather x1, waiting for transfers between devices: 34.9 us -> 40.8 us  [carried_in(): gathered = lax.all_gather(part, axis)]
  transfers between devices with their start and end apart: 2 -> 8, of which waited for: 2 -> 8; matrix products, arithmetic and copies ran while one was open for 2% -> 3% of each run, Pallas kernels for 0% -> 0%
where the time goes in v1:
time: 361 us; the launch traced here: 360 us
  other arithmetic  169 us (47%)
  waiting for transfers between devices  84 us (23%)
  local copies, waits for them, and re-layouts  46.2 us (13%)
  matrix products  29.3 us (8%)
  starting transfers between devices  16.8 us (5%)
  between operations  13.9 us (4%)
    another operation x7, other arithmetic, solve_single(): jax.scipy.linalg.solve_triangular(matrix, target, lower=True, unit_diagon...  161 us
    ppermute x7, waiting for transfers between devices, fill_spot(): lax.ppermute(cards[-1], dev_axis, [(kk, (kk + 1) % slots) for kk in range...  43.2 us
    all_gather x1, waiting for transfers between devices, carried_in(): gathered = lax.all_gather(part, axis)  40.8 us
    ppermute x7, starting transfers between devices, fill_spot(): lax.ppermute(cards[-1], dev_axis, [(kk, (kk + 1) % slots) for kk in range...  16.8 us
    unnamed x50, local copies, waits for them, and re-layouts  10.2 us
    squeeze x8, local copies, waits for them, and re-layouts, ordered_prefix(): closing, before_all = lax.scan(ordered_accumulate, identity_pair(), stacked)  8.68 us
    another operation x6, local copies, waits for them, and re-layouts  8.21 us
    dot_general x13, matrix products, compose(): jnp.einsum('...de,...ef->...df', second_trans, first_pair, precision=high...  7.63 us
  transfers between devices with their start and end apart: 8, of which 8 were waited for; matrix products, arithmetic and copies ran while one was open for 3% of the time, Pallas kernels for 0%

profile of v1, /device:TPU:25, one launch (start us, length us, event | category | flops | bytes accessed | tf_op | source)
XLA Modules:
  0.0 359.7 jit_solution(6387729786878931860)
XLA Ops:
  6.6 1.8 multiply_reduce_fusion
  11.3 2.3 select_add_fusion
  15.2 8.2 %while.38 = (s32[]{:T(128)}, f32[8,256,256]{2,1,0:T(8,128)}, s32[2,2]{1,0:T(2,128)S(1)}, f32[2,8,128,128]{3,2,0,1:T(8,128)}, s32[]{:T(128)}) while((s32[]{:T(128)}, f32[8,256,256]{2,1,0:T(8,128)}, s32[2,2]{1,0:T(2,128)S(1)}, f32[2,8,128,128]{3,2,0,1:T(8,128)}, s32[]{:T(128)}) %tuple.63), condition=%wide.while_cond, body=%wide.while_body.sunk | while | flops 2 | bytes 1050209 | solution.py:42
  15.8 3.6 %bitcast_dynamic-update-slice_fusion.8 = f32[2,8,128,128]{3,2,0,1:T(8,128)} fusion(f32[2,8,128,128]{3,2,0,1:T(8,128)} %get-tuple-element.250, s32[]{:T(128)} %get-tuple-element.247, f32[8,256,256]{2,1,0:T(8,128)} %get-tuple-element.253, s32[]{:T(128)} %bitcast.102, s32[]{:T(128)} %bitcast.103), kind=kLoop, calls=%fused_computation.11.clone.1 | loop fusion | bytes 1050112 | tf_op jit(solution)/shard_map/vmap(jit(_solve_triangular))/triangular_solve
  20.0 3.4 bitcast_dynamic-update-slice_fusion.8
  23.4 158.6 %custom-call.4 = f32[8,2,128,128]{2,3,1,0:T(8,128)} custom-call(f32[8,2,128,128]{3,2,1,0:T(8,128)} %bitcast.122), custom_call_target="InvertDiagBlocksLowerTriangular" | custom-call | tf_op jit(solution)/shard_map/vmap(jit(_solve_triangular))/triangular_solve | solution.py:42
  184.9 2.1 convolution_subtract_fusion
  188.4 2.2 fusion.13
  190.6 2.2 convolution_subtract_fusion.2
  194.2 5.6 %while.35 = (s32[]{:T(128)}, f32[4,128,256]{2,1,0:T(8,128)S(1)}, f32[2,4,128,256]{3,2,1,0:T(8,128)}, f32[2,4,128,256]{2,3,1,0:T(8,128)}, s32[]{:T(128)}) while((s32[]{:T(128)}, f32[4,128,256]{2,1,0:T(8,128)S(1)}, f32[2,4,128,256]{3,2,1,0:T(8,128)}, f32[2,4,128,256]{2,3,1,0:T(8,128)}, s32[]{:T(128)}) %tuple.66), condition=%wide.region_2.3_spmd, body=%wide.region_1.2_spmd.sunk | while | flops 201457664 | bytes 6292033 | solution.py:113
  199.8 1.8 collective-permute-start
  201.6 6.1 %collective-permute-done = f32[1,4,128,256]{3,2,1,0:T(8,128)S(1)} collective-permute-done((f32[1,4,128,256]{3,2,1,0:T(8,128)S(1)}, f32[1,4,128,256]{3,2,1,0:T(8,128)S(1)}, u32[]{:S(2)}, u32[]{:S(2)}) %collective-permute-start) | collective-permute-done | bytes 524320 | tf_op jit(solution)/shard_map/ppermute | solution.py:18
  207.7 2.5 collective-permute-start.1
  210.2 6.1 %collective-permute-done.1 = f32[1,4,128,256]{3,2,1,0:T(8,128)S(1)} collective-permute-done((f32[1,4,128,256]{3,2,1,0:T(8,128)S(1)}, f32[1,4,128,256]{3,2,1,0:T(8,128)S(1)}, u32[]{:S(2)}, u32[]{:S(2)}) %collective-permute-start.1) | collective-permute-done | bytes 524320 | tf_op jit(solution)/shard_map/ppermute | solution.py:18
  216.4 2.5 collective-permute-start.2
  218.8 6.1 %collective-permute-done.2 = f32[1,4,128,256]{3,2,1,0:T(8,128)S(1)} collective-permute-done((f32[1,4,128,256]{3,2,1,0:T(8,128)S(1)}, f32[1,4,128,256]{3,2,1,0:T(8,128)S(1)}, u32[]{:S(2)}, u32[]{:S(2)}) %collective-permute-start.2) | collective-permute-done | bytes 524320 | tf_op jit(solution)/shard_map/ppermute | solution.py:18
  225.8 2.5 collective-permute-start.3
  228.2 6.1 %collective-permute-done.3 = f32[1,4,128,256]{3,2,1,0:T(8,128)S(1)} collective-permute-done((f32[1,4,128,256]{3,2,1,0:T(8,128)S(1)}, f32[1,4,128,256]{3,2,1,0:T(8,128)S(1)}, u32[]{:S(2)}, u32[]{:S(2)}) %collective-permute-start.3) | collective-permute-done | bytes 524320 | tf_op jit(solution)/shard_map/ppermute | solution.py:18
  235.2 2.5 collective-permute-start.4
  237.7 6.1 %collective-permute-done.4 = f32[1,4,128,256]{3,2,1,0:T(8,128)S(1)} collective-permute-done((f32[1,4,128,256]{3,2,1,0:T(8,128)S(1)}, f32[1,4,128,256]{3,2,1,0:T(8,128)S(1)}, u32[]{:S(2)}, u32[]{:S(2)}) %collective-permute-start.4) | collective-permute-done | bytes 524320 | tf_op jit(solution)/shard_map/ppermute | solution.py:18
  244.6 2.5 collective-permute-start.5
  247.1 6.1 %collective-permute-done.5 = f32[1,4,128,256]{3,2,1,0:T(8,128)} collective-permute-done((f32[1,4,128,256]{3,2,1,0:T(8,128)S(1)}, f32[1,4,128,256]{3,2,1,0:T(8,128)}, u32[]{:S(2)}, u32[]{:S(2)}) %collective-permute-start.5) | collective-permute-done | bytes 524320 | tf_op jit(solution)/shard_map/ppermute | solution.py:18
  253.2 2.6 collective-permute-start.6
  255.8 6.4 %collective-permute-done.6 = f32[1,4,128,256]{3,2,1,0:T(8,128)} collective-permute-done((f32[1,4,128,256]{3,2,1,0:T(8,128)}, f32[1,4,128,256]{3,2,1,0:T(8,128)}, u32[]{:S(2)}, u32[]{:S(2)}) %collective-permute-start.6) | collective-permute-done | bytes 524320 | tf_op jit(solution)/shard_map/ppermute | solution.py:18
  269.4 2.3 constant_dynamic-slice_fusion.2
  271.7 21.0 %while.36 = (s32[]{:T(128)}, f32[4,128,256]{2,1,0:T(8,128)S(1)}, f32[8,4,128,256]{3,2,1,0:T(8,128)}, f32[8,4,128,256]{3,2,1,0:T(8,128)}, s32[]{:T(128)}) while((s32[]{:T(128)}, f32[4,128,256]{2,1,0:T(8,128)S(1)}, f32[8,4,128,256]{3,2,1,0:T(8,128)}, f32[8,4,128,256]{3,2,1,0:T(8,128)}, s32[]{:T(128)}) %tuple.78), condition=%wide.region_4.5_spmd, body=%wide.region_3.4_spmd.sunk | while | flops 201457664 | bytes 5243457 | solution.py:84
  294.4 3.1 convolution_subtract_fusion.1
  297.5 1.7 fusion.19
  299.2 1.7 fusion.23
  300.9 1.9 fusion.5
  303.9 40.8 %all-gather.3.cloned.1.call-done = f32[16,128,256]{2,1,0:T(8,128)} async-done(((f32[4,128,256]{2,1,0:T(8,128)}), f32[16,128,256]{2,1,0:T(8,128)}) %all-gather.3.cloned.1.call-update) | async-done | bytes 2097168 | tf_op jit(solution)/shard_map/all_gather | solution.py:27
  344.6 5.3 %while.37 = (s32[]{:T(128)}, f32[4,128,256]{2,1,0:T(8,128)S(1)}, s32[]{:T(128)}, f32[4,4,128,256]{3,2,1,0:T(8,128)}, s32[]{:T(128)}, /*index=5*/s32[]{:T(128)}, s32[]{:T(128)}) while((s32[]{:T(128)}, f32[4,128,256]{2,1,0:T(8,128)S(1)}, s32[]{:T(128)}, f32[4,4,128,256]{3,2,1,0:T(8,128)}, s32[]{:T(128)}, /*index=5*/s32[]{:T(128)}, ...), condition=%wide.region_6.7_spmd, body=%wide.region_5.6_spmd.sunk | while | flops 201457664 | bytes 4194419 | solution.py:33
  (155 shorter events, 57.5 us)
Async XLA Ops:
  6.5 343.4 %copy-start = (f32[4,128,128]{2,1,0:T(8,128)S(1)}, f32[4,128,128]{2,1,0:T(8,128)}, u32[]{:S(2)}) copy-start(f32[4,128,128]{2,1,0:T(8,128)} %param.15) | copy-start | bytes 786436
  6.5 338.1 %all-gather.3.cloned.1.call-start = ((), (), s32[]{:S(2)}) async-start(), calls=%async_computation | async-start | bytes 2621440 | tf_op jit(solution)/shard_map/all_gather | solution.py:27
  13.6 168.5 %copy-start.15 = (bf16[1,256,2,4,128]{4,3,2,1,0:T(4,128)(2,1)S(1)}, bf16[1,256,2,4,128]{4,3,2,1,0:T(4,128)(2,1)}, u32[]{:S(2)}) copy-start(bf16[1,256,2,4,128]{4,3,2,1,0:T(4,128)(2,1)} %param.13) | copy-start | bytes 1572868
  182.1 1.8 copy-start.13
  188.4 2.2 copy-start.5
  193.0 62.8 %copy-start.1 = (f32[4,128,256]{2,1,0:T(8,128)}, f32[4,128,256]{2,1,0:T(8,128)S(1)}, u32[]{:S(2)}) copy-start(f32[4,128,256]{2,1,0:T(8,128)S(1)} %concatenate.29) | copy-start | bytes 1572868
  199.8 7.9 %collective-permute-start = (f32[1,4,128,256]{3,2,1,0:T(8,128)S(1)}, f32[1,4,128,256]{3,2,1,0:T(8,128)S(1)}, u32[]{:S(2)}, u32[]{:S(2)}) collective-permute-start(f32[1,4,128,256]{3,2,1,0:T(8,128)S(1)} %bitcast.106), channel_id=1, source_target_pairs={{0,4},{4,8},{8,12},{12,16},{16,20},{20,24},{24,28},{28,0},{1,5},{5... | collective-permute-start | bytes 1572872 | tf_op jit(solution)/shard_map/ppermute | solution.py:18
  207.7 8.6 %collective-permute-start.1 = (f32[1,4,128,256]{3,2,1,0:T(8,128)S(1)}, f32[1,4,128,256]{3,2,1,0:T(8,128)S(1)}, u32[]{:S(2)}, u32[]{:S(2)}) collective-permute-start(f32[1,4,128,256]{3,2,1,0:T(8,128)S(1)} %collective-permute-done), channel_id=1, source_target_pairs={{0,4},{4,8},{8,12},{12,16},{16,20},{20,24},{24,28},{28,0},{1,5},{5... | collective-permute-start | bytes 1572872 | tf_op jit(solution)/shard_map/ppermute | solution.py:18
  216.4 8.6 %collective-permute-start.2 = (f32[1,4,128,256]{3,2,1,0:T(8,128)S(1)}, f32[1,4,128,256]{3,2,1,0:T(8,128)S(1)}, u32[]{:S(2)}, u32[]{:S(2)}) collective-permute-start(f32[1,4,128,256]{3,2,1,0:T(8,128)S(1)} %collective-permute-done.1), channel_id=1, source_target_pairs={{0,4},{4,8},{8,12},{12,16},{16,20},{20,24},{24,28},{28,0},{1,5},{5... | collective-permute-start | bytes 1572872 | tf_op jit(solution)/shard_map/ppermute | solution.py:18
  225.0 0.8 copy-start.7
  225.8 8.6 %collective-permute-start.3 = (f32[1,4,128,256]{3,2,1,0:T(8,128)S(1)}, f32[1,4,128,256]{3,2,1,0:T(8,128)S(1)}, u32[]{:S(2)}, u32[]{:S(2)}) collective-permute-start(f32[1,4,128,256]{3,2,1,0:T(8,128)S(1)} %collective-permute-done.2), channel_id=1, source_target_pairs={{0,4},{4,8},{8,12},{12,16},{16,20},{20,24},{24,28},{28,0},{1,5},{5... | collective-permute-start | bytes 1572872 | tf_op jit(solution)/shard_map/ppermute | solution.py:18
  234.4 0.8 copy-start.9
  235.2 8.6 %collective-permute-start.4 = (f32[1,4,128,256]{3,2,1,0:T(8,128)S(1)}, f32[1,4,128,256]{3,2,1,0:T(8,128)S(1)}, u32[]{:S(2)}, u32[]{:S(2)}) collective-permute-start(f32[1,4,128,256]{3,2,1,0:T(8,128)S(1)} %collective-permute-done.3), channel_id=1, source_target_pairs={{0,4},{4,8},{8,12},{12,16},{16,20},{20,24},{24,28},{28,0},{1,5},{5... | collective-permute-start | bytes 1572872 | tf_op jit(solution)/shard_map/ppermute | solution.py:18
  243.8 0.8 copy-start.11
  244.6 8.6 %collective-permute-start.5 = (f32[1,4,128,256]{3,2,1,0:T(8,128)S(1)}, f32[1,4,128,256]{3,2,1,0:T(8,128)}, u32[]{:S(2)}, u32[]{:S(2)}) collective-permute-start(f32[1,4,128,256]{3,2,1,0:T(8,128)S(1)} %collective-permute-done.4), channel_id=1, source_target_pairs={{0,4},{4,8},{8,12},{12,16},{16,20},{20,24},{24,28},{28,0},{1,5},{5... | collective-permute-start | bytes 1572872 | tf_op jit(solution)/shard_map/ppermute | solution.py:18
  253.2 9.0 %collective-permute-start.6 = (f32[1,4,128,256]{3,2,1,0:T(8,128)}, f32[1,4,128,256]{3,2,1,0:T(8,128)}, u32[]{:S(2)}, u32[]{:S(2)}) collective-permute-start(f32[1,4,128,256]{3,2,1,0:T(8,128)} %collective-permute-done.5), channel_id=1, source_target_pairs={{0,4},{4,8},{8,12},{12,16},{16,20},{20,24},{24,28},{28,0},{1,5},{5... | collective-permute-start | bytes 1572872 | tf_op jit(solution)/shard_map/ppermute | solution.py:18
  255.8 10.9 %copy-start.8 = (f32[1,4,128,256]{3,2,1,0:T(8,128)S(1)}, f32[1,4,128,256]{3,2,1,0:T(8,128)}, u32[]{:S(2)}) copy-start(f32[1,4,128,256]{3,2,1,0:T(8,128)} %copy-done.7) | copy-start | bytes 1572868
  264.4 4.7 %copy-start.12 = (f32[1,4,128,256]{3,2,1,0:T(8,128)S(1)}, f32[1,4,128,256]{3,2,1,0:T(8,128)}, u32[]{:S(2)}) copy-start(f32[1,4,128,256]{3,2,1,0:T(8,128)} %copy-done.11) | copy-start | bytes 1572868
  265.5 3.6 copy-start.10
  269.3 2.3 copy-start.4
  271.7 21.9 %copy-start.14 = (bf16[1,256,4,128]{3,2,1,0:T(4,128)(2,1)S(1)}, bf16[1,256,4,128]{3,2,1,0:T(4,128)(2,1)}, u32[]{:S(2)}) copy-start(bf16[1,256,4,128]{3,2,1,0:T(4,128)(2,1)} %param.11) | copy-start | bytes 786436
  292.7 0.8 copy-start.3
  293.6 7.3 %copy-start.6 = (f32[8,256,256]{2,1,0:T(8,128)S(1)}, f32[8,256,256]{2,1,0:T(8,128)}, u32[]{:S(2)}) copy-start(f32[8,256,256]{2,1,0:T(8,128)} %copy-done.5) | copy-start | bytes 6291460
  297.5 47.2 %copy-start.2 = (f32[4,128,256]{2,1,0:T(8,128)S(1)}, f32[4,128,256]{2,1,0:T(8,128)}, u32[]{:S(2)}) copy-start(f32[4,128,256]{2,1,0:T(8,128)} %copy-done.1) | copy-start | bytes 1572868
  344.6 7.1 %copy-start.16 = (f32[4,128]{1,0:T(4,128)S(1)}, f32[4,128]{1,0:T(4,128)}, u32[]{:S(2)}) copy-start(f32[4,128]{1,0:T(4,128)} %param.14) | copy-start | bytes 6148
Sparse Core Ops, SparseCore 0:
  293.7 50.9 all-gather.2
